TPU v7x, 32 devices: a whole 2x2x4 slice. The times are simulated.
32 devices in a mesh: dp: 8 (over y, x, core), sp: 4 (over z).
Axes of the slice: x: 2, y: 2, z: 4, core: 2. Of those that a mesh axis runs over, the one named last changes fastest.
Arguments:
- hidden_in: bfloat16 [32, 1024, 768], P('dp', 'sp'), may hold values from -6 to 6
- time_embed: bfloat16 [32, 128], P('dp'), may hold values from -6 to 6
- ada_weight: bfloat16 [128, 4608], replicated, may hold values from -0.25 to 0.25
- ada_bias: bfloat16 [4608], replicated, may hold values from -1.5 to 1.5
- attn_gain: bfloat16 [768], replicated, may hold values from 0.25 to 1.75
- query_key_value_matrix: bfloat16 [768, 2304], replicated, may hold values from -0.21875 to 0.21875
- attention_output_matrix: bfloat16 [768, 768], replicated, may hold values from -1.75 to 1.75
- mlp_gain: bfloat16 [768], replicated, may hold values from 0.25 to 1.75
- up_projection_matrix: bfloat16 [768, 3072], replicated, may hold values from -0.21875 to 0.21875
- up_bias: bfloat16 [3072], replicated, may hold values from -3 to 3
- down_projection_matrix: bfloat16 [3072, 768], replicated, may hold values from -0.109375 to 0.109375
- down_bias: bfloat16 [768], replicated, may hold values from -3 to 3
- out_cotangent: bfloat16 [32, 1024, 768], P('dp', 'sp'), may hold values from -6 to 6
Outputs:
- output: bfloat16 [32, 1024, 768], P('dp', 'sp')
- hidden_grad: float32 [32, 1024, 768], P('dp', 'sp')
- time_grad: float32 [32, 128], P('dp')
- ada_weight_grad: float32 [128, 4608], P('sp')
- ada_bias_grad: float32 [4608], P('sp')
- attn_gain_grad: float32 [768], P('sp')
- qkv_weight_grad: float32 [768, 2304], P('sp')
- proj_weight_grad: float32 [768, 768], P('sp')
- mlp_gain_grad: float32 [768], P('sp')
- up_weight_grad: float32 [768, 3072], P('sp')
- up_bias_grad: float32 [3072], P('sp')
- down_weight_grad: float32 [3072, 768], P('sp')
- down_bias_grad: float32 [768], P('sp')
All inputs are finite; a program needn't handle non-finite values.
Results may differ from a plain program's by a relative error of at most 0.012.
The roundings to bfloat16 on the way count: a program that leaves them out, or rounds other values in their place, can miss the bound.
Values may be sent and summed in bfloat16 or wider, within the bound.
No kernel may reach another device: no remote copies, remote signals or barrier semaphores. Data moves between devices by JAX's collectives and lax.ppermute only.
A program may use at most 192 MiB of HBM per device.

v0:
```python
import jax
import jax.numpy as jnp
from jax import lax
from jax.sharding import PartitionSpec as P

HEAD_DIM = 64
highest = lax.Precision.HIGHEST
epsilon = 1e-05


def rope_tables(length, columns):
    half_width = columns // 2
    frequency = 10000.0 ** (-(jnp.arange(half_width, dtype=jnp.float32) * 2.0 / columns))
    angles = jnp.arange(length, dtype=jnp.float32)[:, None] * frequency[None, :]
    cos_table = jnp.cos(angles)
    sin_table = jnp.sin(angles)
    cos_table = jnp.concatenate([cos_table, cos_table], axis=-1)[:, None, :]
    sin_table = jnp.concatenate([sin_table, sin_table], axis=-1)[:, None, :]
    return (cos_table, sin_table)


def rotary(values, cos_table, sin_table):
    half_width = values.shape[-1] // 2
    turned = jnp.concatenate([-values[..., half_width:], values[..., :half_width]], axis=-1)
    return values * cos_table + turned * sin_table


def unrotary(gradients, cos_table, sin_table):
    half_width = gradients.shape[-1] // 2
    scaled = gradients * sin_table
    turned = jnp.concatenate([scaled[..., half_width:], -scaled[..., :half_width]], axis=-1)
    return gradients * cos_table + turned


def gelu_tanh(values):
    return jax.nn.gelu(values, approximate=True)


def norm_forward(values):
    center = values - jnp.mean(values, axis=-1, keepdims=True)
    inverse = lax.rsqrt(jnp.mean(center * center, axis=-1, keepdims=True) + epsilon)
    return (center * inverse, inverse)


def norm_backward(grad_normed, normed, inverse):
    first = jnp.mean(grad_normed, axis=-1, keepdims=True)
    second = jnp.mean(grad_normed * normed, axis=-1, keepdims=True)
    return inverse * (grad_normed - first - normed * second)


def rotate_single(single, cos_table, sin_table):
    length = single.shape[0]
    heads_here = single.shape[2] // HEAD_DIM
    shaped = single.astype(jnp.float32).reshape(length, 3, heads_here, HEAD_DIM)
    queries = rotary(shaped[:, 0], cos_table, sin_table).astype(jnp.bfloat16).reshape(length, -1)
    rotated_keys = (
        rotary(shaped[:, 1], cos_table, sin_table).astype(jnp.bfloat16).reshape(length, -1)
    )
    return jnp.stack([queries, rotated_keys, single[:, 2]], axis=1)


def attend_single(rotated):
    length = rotated.shape[0]
    heads_here = rotated.shape[2] // HEAD_DIM
    queries = rotated[:, 0].reshape(length, heads_here, HEAD_DIM)
    rotated_keys = rotated[:, 1].reshape(length, heads_here, HEAD_DIM)
    values = rotated[:, 2].reshape(length, heads_here, HEAD_DIM)
    scores = jnp.einsum(
        "qhd,khd->hqk", queries, rotated_keys, preferred_element_type=jnp.float32
    ) * HEAD_DIM ** (-0.5)
    probabilities = jax.nn.softmax(scores, axis=-1).astype(jnp.bfloat16)
    mixed_heads = jnp.einsum(
        "hqk,khd->qhd", probabilities, values, preferred_element_type=jnp.float32
    )
    return mixed_heads.reshape(length, -1).astype(jnp.bfloat16)


def attend_items(several):
    cos_table, sin_table = rope_tables(several.shape[1], HEAD_DIM)

    def one_single(single):
        rotated = rotate_single(single, cos_table, sin_table)
        return (attend_single(rotated), rotated)

    return lax.map(one_single, several)


def backward_single(rotated, grad_mixed, cos_table, sin_table):
    length = rotated.shape[0]
    heads_here = rotated.shape[2] // HEAD_DIM
    queries = rotated[:, 0].reshape(length, heads_here, HEAD_DIM)
    rotated_keys = rotated[:, 1].reshape(length, heads_here, HEAD_DIM)
    values = rotated[:, 2].reshape(length, heads_here, HEAD_DIM)
    grad_heads = grad_mixed.reshape(length, heads_here, HEAD_DIM)
    scale_factor = HEAD_DIM ** (-0.5)
    scores = (
        jnp.einsum("qhd,khd->hqk", queries, rotated_keys, preferred_element_type=jnp.float32)
        * scale_factor
    )
    probabilities = jax.nn.softmax(scores, axis=-1)
    probs_low = probabilities.astype(jnp.bfloat16)
    grad_values = jnp.einsum(
        "hqk,qhd->khd", probs_low, grad_heads, preferred_element_type=jnp.float32
    )
    grad_probs = jnp.einsum("qhd,khd->hqk", grad_heads, values, preferred_element_type=jnp.float32)
    row_terms = jnp.sum(probabilities * grad_probs, axis=-1, keepdims=True)
    grad_scores = (probabilities * (grad_probs - row_terms)).astype(jnp.bfloat16)
    grad_queries = (
        jnp.einsum("hqk,khd->qhd", grad_scores, rotated_keys, preferred_element_type=jnp.float32)
        * scale_factor
    )
    grad_keys = (
        jnp.einsum("hqk,qhd->khd", grad_scores, queries, preferred_element_type=jnp.float32)
        * scale_factor
    )
    grad_queries = unrotary(grad_queries, cos_table, sin_table)
    grad_keys = unrotary(grad_keys, cos_table, sin_table)
    stacked = jnp.stack(
        [
            grad_queries.reshape(length, -1),
            grad_keys.reshape(length, -1),
            grad_values.reshape(length, -1),
        ],
        axis=1,
    )
    return stacked.astype(jnp.bfloat16)


def body(
    hidden_in,
    time_embed,
    ada_weight,
    ada_bias,
    attn_gain,
    query_key_value_matrix,
    attention_output_matrix,
    mlp_gain,
    up_projection_matrix,
    up_bias,
    down_projection_matrix,
    down_bias,
    out_cotangent,
):
    seq_count, local_len, width = hidden_in.shape
    residual = hidden_in.astype(jnp.float32)
    ada_full = ada_weight.astype(jnp.float32)
    timing = time_embed.astype(jnp.float32)
    modulation = jnp.dot(timing, ada_full, precision=highest) + ada_bias.astype(jnp.float32)
    shift_attn, scale_attn, gate_attn, shift_mlp, scale_mlp, gate_mlp = jnp.split(
        modulation[:, None, :], 6, axis=-1
    )
    gain_attn = attn_gain.astype(jnp.float32)
    gain_mlp = mlp_gain.astype(jnp.float32)
    normed_attn, inverse_attn = norm_forward(residual)
    attention_modulated_input = (normed_attn * gain_attn * (1.0 + scale_attn) + shift_attn).astype(
        jnp.bfloat16
    )
    qkv_seq = jnp.einsum(
        "tig,gn->tin",
        attention_modulated_input,
        query_key_value_matrix,
        preferred_element_type=jnp.float32,
    )
    qkv_seq = qkv_seq.astype(jnp.bfloat16).reshape(seq_count, local_len, 3, width)
    mixed_heads, kept_heads = attend_items(
        lax.all_to_all(qkv_seq, "sp", split_axis=3, concat_axis=1, tiled=True)
    )
    attention_mixed_sequence = lax.all_to_all(
        mixed_heads, "sp", split_axis=1, concat_axis=2, tiled=True
    )
    projected = jnp.einsum(
        "tig,gn->tin",
        attention_mixed_sequence,
        attention_output_matrix,
        preferred_element_type=jnp.float32,
    )
    middle = residual + gate_attn * projected
    normed_mlp, inverse_mlp = norm_forward(middle)
    feedforward_modulated_input = (normed_mlp * gain_mlp * (1.0 + scale_mlp) + shift_mlp).astype(
        jnp.bfloat16
    )
    pre_act = jnp.einsum(
        "xac,cz->xaz",
        feedforward_modulated_input,
        up_projection_matrix,
        preferred_element_type=jnp.float32,
    ) + up_bias.astype(jnp.float32)
    activated_f, gelu_pullback = jax.vjp(gelu_tanh, pre_act)
    gelu_activation = activated_f.astype(jnp.bfloat16)
    down_out = jnp.einsum(
        "ngw,wo->ngo", gelu_activation, down_projection_matrix, preferred_element_type=jnp.float32
    ) + down_bias.astype(jnp.float32)
    output = (middle + gate_mlp * down_out).astype(jnp.bfloat16)
    grad_out = out_cotangent.astype(jnp.float32)
    grad_gate_mlp = jnp.sum(grad_out * down_out, axis=1)
    down_output_gradient = (gate_mlp * grad_out).astype(jnp.bfloat16)
    grad_down_bias = jnp.sum(down_output_gradient.astype(jnp.float32), axis=(0, 1))
    grad_down_weight = jnp.einsum(
        "qpj,qpi->ji", gelu_activation, down_output_gradient, preferred_element_type=jnp.float32
    )
    activation_gradient = jnp.einsum(
        "eoa,ta->eot",
        down_output_gradient,
        down_projection_matrix,
        preferred_element_type=jnp.float32,
    )
    preactivation_gradient = gelu_pullback(activation_gradient)[0].astype(jnp.bfloat16)
    grad_up_bias = jnp.sum(preactivation_gradient.astype(jnp.float32), axis=(0, 1))
    grad_up_weight = jnp.einsum(
        "rqm,rqc->mc",
        feedforward_modulated_input,
        preactivation_gradient,
        preferred_element_type=jnp.float32,
    )
    grad_mod_mlp = jnp.einsum(
        "qbz,nz->qbn",
        preactivation_gradient,
        up_projection_matrix,
        preferred_element_type=jnp.float32,
    )
    grad_shift_mlp = jnp.sum(grad_mod_mlp, axis=1)
    grad_scale_mlp = jnp.sum(grad_mod_mlp * normed_mlp * gain_mlp, axis=1)
    grad_mlp_gain = jnp.sum(grad_mod_mlp * (1.0 + scale_mlp) * normed_mlp, axis=(0, 1))
    grad_middle = grad_out + norm_backward(
        grad_mod_mlp * gain_mlp * (1.0 + scale_mlp), normed_mlp, inverse_mlp
    )
    grad_gate_attn = jnp.sum(grad_middle * projected, axis=1)
    projection_output_gradient = (gate_attn * grad_middle).astype(jnp.bfloat16)
    grad_proj_weight = jnp.einsum(
        "kuv,kuf->vf",
        attention_mixed_sequence,
        projection_output_gradient,
        preferred_element_type=jnp.float32,
    )
    grad_mixed = jnp.einsum(
        "oam,ym->oay",
        projection_output_gradient,
        attention_output_matrix,
        preferred_element_type=jnp.float32,
    ).astype(jnp.bfloat16)
    grad_heads = lax.all_to_all(grad_mixed, "sp", split_axis=2, concat_axis=1, tiled=True)
    cos_table, sin_table = rope_tables(grad_heads.shape[1], HEAD_DIM)

    def kept_pair(pair):
        return backward_single(pair[0], pair[1], cos_table, sin_table)

    grad_qkv_heads = lax.map(kept_pair, (kept_heads, grad_heads))
    query_key_value_gradient = lax.all_to_all(
        grad_qkv_heads, "sp", split_axis=1, concat_axis=3, tiled=True
    ).reshape(seq_count, local_len, 3 * width)
    grad_qkv_weight = jnp.einsum(
        "kuv,kuf->vf",
        attention_modulated_input,
        query_key_value_gradient,
        preferred_element_type=jnp.float32,
    )
    grad_mod_attn = jnp.einsum(
        "oam,ym->oay",
        query_key_value_gradient,
        query_key_value_matrix,
        preferred_element_type=jnp.float32,
    )
    grad_shift_attn = jnp.sum(grad_mod_attn, axis=1)
    grad_scale_attn = jnp.sum(grad_mod_attn * normed_attn * gain_attn, axis=1)
    grad_attn_gain = jnp.sum(grad_mod_attn * (1.0 + scale_attn) * normed_attn, axis=(0, 1))
    hidden_grad = grad_middle + norm_backward(
        grad_mod_attn * gain_attn * (1.0 + scale_attn), normed_attn, inverse_attn
    )
    grad_modulation = jnp.concatenate(
        [
            grad_shift_attn,
            grad_scale_attn,
            grad_gate_attn,
            grad_shift_mlp,
            grad_scale_mlp,
            grad_gate_mlp,
        ],
        axis=-1,
    )
    full_modulation = lax.psum(grad_modulation.astype(jnp.bfloat16), "sp").astype(jnp.float32)
    time_grad = jnp.dot(full_modulation, ada_full.T, precision=highest)
    grad_ada_weight = jnp.dot(timing.T, grad_modulation, precision=highest)
    grad_ada_bias = jnp.sum(grad_modulation, axis=0)
    shards = (
        lax.psum_scatter(grad_ada_weight, "sp", scatter_dimension=0, tiled=True),
        lax.psum_scatter(grad_ada_bias, "sp", scatter_dimension=0, tiled=True),
        lax.psum_scatter(grad_attn_gain, "sp", scatter_dimension=0, tiled=True),
        lax.psum_scatter(grad_qkv_weight, "sp", scatter_dimension=0, tiled=True),
        lax.psum_scatter(grad_proj_weight, "sp", scatter_dimension=0, tiled=True),
        lax.psum_scatter(grad_mlp_gain, "sp", scatter_dimension=0, tiled=True),
        lax.psum_scatter(grad_up_weight, "sp", scatter_dimension=0, tiled=True),
        lax.psum_scatter(grad_up_bias, "sp", scatter_dimension=0, tiled=True),
        lax.psum_scatter(grad_down_weight, "sp", scatter_dimension=0, tiled=True),
        lax.psum_scatter(grad_down_bias, "sp", scatter_dimension=0, tiled=True),
    )
    summed = lax.psum(
        (
            shards[0],
            shards[1],
            shards[2],
            shards[3],
            shards[4],
            shards[5],
            shards[6],
            shards[7],
            shards[8],
            shards[9],
        ),
        "dp",
    )
    return (
        output,
        hidden_grad,
        time_grad,
        summed[0],
        summed[1],
        summed[2],
        summed[3],
        summed[4],
        summed[5],
        summed[6],
        summed[7],
        summed[8],
        summed[9],
    )


def solution(mesh):
    return jax.shard_map(
        body,
        mesh=mesh,
        in_specs=(
            P("dp", "sp", None),
            P("dp", None),
            P(),
            P(),
            P(),
            P(),
            P(),
            P(),
            P(),
            P(),
            P(),
            P(),
            P("dp", "sp", None),
        ),
        out_specs=(
            P("dp", "sp", None),
            P("dp", "sp", None),
            P("dp", None),
            P("sp", None),
            P("sp"),
            P("sp"),
            P("sp", None),
            P("sp", None),
            P("sp"),
            P("sp", None),
            P("sp"),
            P("sp", None),
            P("sp"),
        ),
        check_vma=False,
    )
```

profile of v0, /device:TPU:0, one launch (start us, length us, event | category | flops | bytes accessed | tf_op | source)
XLA Modules:
  0.0 1487.4 jit_solution(7449121573997723435)
XLA Ops:
  13.8 5.9 convolution_convert_fusion
  19.7 6.7 copy.121
  26.4 8.1 copy.122
  34.5 6.5 all-to-all-start
  42.4 103.3 %all-to-all-done = bf16[4,256,3,768]{1,0,2,3:T(4,128)(2,1)} async-done(((bf16[4,256,3,768]{1,0,2,3:T(4,128)(2,1)}), bf16[4,256,3,768]{1,0,2,3:T(4,128)(2,1)}, u32[]{:S(2)}, u32[]{:S(2)}) %all-to-all-start) | async-done | bytes 4718624 | tf_op jit(solution)/shard_map/all_to_all | solution.py:166
  154.2 99.2 %while.22 = (s32[]{:T(128)}, bf16[4,1024,192]{1,2,0:T(8,128)(2,1)}, bf16[4,1024,3,192]{1,3,2,0:T(8,128)(2,1)}, bf16[4,1024,3,192]{1,3,2,0:T(8,128)(2,1)}, f32[10...) while((s32[]{:T(128)}, bf16[4,1024,192]{1,2,0:T(8,128)(2,1)}, ...), condition=%wide.region_5.6_spmd, body=%wide.region_2.5_spmd.sunk | while | flops 828703744 | bytes 63856824 | solution.py:85
  162.7 9.6 fusion.151
  172.3 5.9 fusion.152
  187.5 9.6 fusion.151
  197.1 5.9 fusion.152
  212.3 9.6 fusion.151
  221.9 5.9 fusion.152
  237.1 9.6 fusion.151
  246.7 5.9 fusion.152
  265.7 44.1 %all-to-all-done.1 = bf16[4,1024,192]{2,0,1:T(4,128)(2,1)} async-done(((bf16[4,1024,192]{2,0,1:T(4,128)(2,1)}), bf16[4,1024,192]{2,0,1:T(4,128)(2,1)}, u32[]{:S(2)}, u32[]{:S(2)}) %all-to-all-start.1) | async-done | bytes 1572896 | tf_op jit(solution)/shard_map/all_to_all | solution.py:168
  318.8 8.2 fusion.44
  327.0 15.7 %convert_reduce_fusion = (f32[3072]{0:T(1024)}, bf16[4,256,3072]{2,1,0:T(8,128)(2,1)S(1)}) fusion(f32[4,256,3072]{2,1,0:T(8,128)} %fusion.44, f32[3072]{0:T(1024)S(1)} %copy-done.40, bf16[3072,768]{1,0:T(8,128)(2,1)} %param.27, bf16[4,256,768]{2,1,0:T(8,128)(2,1)S(1)} %copy-done.49, f32[4,768]{1,0:T(4,128)S(1)} %copy-done.38), kind=kOutput, calls=%fused_computation.65 | convolution fusion | flops 4906546176 | bytes 25202688 | tf_op jit(solution)/shard_map/eoa,ta->eot/dot_general | solution.py:201
  342.8 13.0 multiply_reduce_fusion.3
  355.8 15.4 %convert_reduce_fusion.2 = (f32[768]{0:T(1024)}, f32[4,768]{1,0:T(4,128)}, bf16[4,256,768]{2,1,0:T(8,128)(2,1)}, f32[4,768]{1,0:T(4,128)}, f32[4,256,768]{2,1,0:T(8,128)S(1)}) fusion(bf16[4,256,768]{2,1,0:T(8,128)(2,1)S(1)} %copy-done.49, f32[4,768]{1,0:T(4,128)S(1)} %copy-done.38, f32[768]{0:T(1024)S(1)} %copy-done.46, ...), kind=kOutput, calls=%fused_computation.111 | convolution fusion | flops 4880589824 | bytes 33117184 | tf_op jit(solution)/shard_map/ngw,wo->ngo/dot_general | solution.py:190
  379.2 40.1 %all_to_all.69 = bf16[4,256,768]{1,0,2:T(4,128)(2,1)S(1)} all-to-all(bf16[4,256,768]{1,0,2:T(4,128)(2,1)} %copy.129), channel_id=1, replica_groups=mesh['dp'=8,'sp'=4] {'sp'}, dimensions={2} | all-to-all | bytes 3145728 | tf_op jit(solution)/shard_map/all_to_all | solution.py:241
  423.7 168.4 %while.23 = (s32[]{:T(128)}, bf16[4,1024,3,192]{1,3,2,0:T(8,128)(2,1)}, bf16[4,1024,3,192]{1,3,2,0:T(8,128)(2,1)}, bf16[4,1024,192]{1,2,0:T(8,128)(2,1)}, f32[10...) while((s32[]{:T(128)}, bf16[4,1024,3,192]{1,3,2,0:T(8,128)(2,1)}, ...), condition=%wide.region_14.15_spmd, body=%wide.region_10.0_spmd.sunk | while | flops 2057041920 | bytes 176759088 | solution.py:247
  429.7 9.6 fusion.167
  439.3 6.9 fusion.168
  453.2 6.7 multiply_convert_fusion.8
  471.8 9.6 fusion.167
  481.4 6.9 fusion.168
  495.3 6.7 multiply_convert_fusion.8
  513.9 9.6 fusion.167
  523.5 6.9 fusion.168
  537.4 6.7 multiply_convert_fusion.8
  556.0 9.6 fusion.167
  565.6 6.9 fusion.168
  579.5 6.7 multiply_convert_fusion.8
  592.1 10.3 copy.132
  602.4 144.0 %all_to_all.70 = bf16[4,1024,3,192]{3,0,2,1:T(4,128)(2,1)} all-to-all(bf16[4,1024,3,192]{3,0,2,1:T(4,128)(2,1)} %copy.132), channel_id=1, replica_groups=mesh['dp'=8,'sp'=4] {'sp'}, dimensions={1} | all-to-all | bytes 9437184 | tf_op jit(solution)/shard_map/all_to_all | solution.py:248
  746.5 10.3 copy.134
  756.8 9.9 fusion.67
  779.2 10.9 convolution_bitcast_fusion.4
  790.8 14.0 convolution_bitcast_fusion.3
  805.5 10.2 convolution_bitcast_fusion.5
  824.4 46.7 %reduce-scatter.10.cloned.1.call-done = f32[192,768]{1,0:T(8,128)} async-done(((f32[768,768]{1,0:T(8,128)}), f32[192,768]{1,0:T(8,128)}) %reduce-scatter.10.cloned.1.call-update) | async-done | bytes 589840 | tf_op jit(solution)/shard_map/reduce_scatter | solution.py:289
  871.2 163.2 %reduce-scatter.12.cloned.1.call-done = f32[192,3072]{1,0:T(8,128)} async-done(((f32[768,3072]{1,0:T(8,128)}), f32[192,3072]{1,0:T(8,128)}) %reduce-scatter.12.cloned.1.call-update) | async-done | bytes 2359312 | tf_op jit(solution)/shard_map/reduce_scatter | solution.py:291
  1034.3 164.4 %reduce-scatter.14.cloned.1.call-done = f32[768,768]{1,0:T(8,128)} async-done(((f32[3072,768]{1,0:T(8,128)}), f32[768,768]{1,0:T(8,128)}) %reduce-scatter.14.cloned.1.call-update) | async-done | bytes 2359312 | tf_op jit(solution)/shard_map/reduce_scatter | solution.py:293
  1198.7 126.5 %reduce-scatter.8.cloned.1.call-done = f32[192,2304]{1,0:T(8,128)} async-done(((f32[768,2304]{1,0:T(8,128)}), f32[192,2304]{1,0:T(8,128)}) %reduce-scatter.8.cloned.1.call-update) | async-done | bytes 1769488 | tf_op jit(solution)/shard_map/reduce_scatter | solution.py:288
  1330.6 19.7 %all-reduce.7 = (f32[4608]{0:T(1024)}, f32[768]{0:T(1024)}, f32[768]{0:T(1024)}, f32[3072]{0:T(1024)}, f32[768]{0:T(1024)}) all-reduce(f32[4608]{0:T(1024)} %get-tuple-element.255, f32[768]{0:T(1024)} %get-tuple-element.162, f32[768]{0:T(1024)} %get-tuple-element.159, ...), channel_id=3, replica_groups=mesh['dp'=8,'sp'=4] {'sp'}, use_global_device_ids=true, to_apply=%region_27.28.clone | all-reduce | flops 9984 | bytes 79872
  1357.1 24.7 %all-reduce.5 = (f32[1152]{0:T(1024)}, f32[192]{0:T(256)}, f32[192]{0:T(256)}, f32[768]{0:T(1024)}, f32[192]{0:T(256)}) all-reduce(f32[1152]{0:T(1024)} %dynamic-slice.1, f32[192]{0:T(256)} %dynamic-slice.3, f32[192]{0:T(256)} %dynamic-slice.5, f32[768]{0:T(1024)} %dynamic-slice.7, ...), channel_id=1, replica_groups=mesh['dp'=8,'sp'=4] {'dp'}, use_global_device_ids=true, to_apply=%region_28.29 | all-reduce | flops 2496 | bytes 19968 | tf_op jit(solution)/shard_map/psum | solution.py:296
  1381.8 17.2 %psum.77 = bf16[4,4608]{1,0:T(4,128)(2,1)} all-reduce(bf16[4,4608]{1,0:T(4,128)(2,1)} %get-tuple-element.256), channel_id=1, replica_groups=mesh['dp'=8,'sp'=4] {'sp'}, use_global_device_ids=true, to_apply=%region_23.24 | all-reduce | flops 18432 | bytes 73728 | tf_op jit(solution)/shard_map/psum | solution.py:280
  1407.9 62.5 %all-reduce.10.cloned.1.call-done = (f32[32,4608]{0,1:T(8,128)}, f32[192,2304]{1,0:T(8,128)}, f32[192,768]{1,0:T(8,128)}, f32[192,3072]{1,0:T(8,128)}, f32[768,768]{1,0:T(8,128)}) async-done(((f32[32,4608]{0,1:T(8,128)}, f32[192,2304]{1,0:T(8,128)}, f32[192,768]{1,0:T(8,128)}, f32[192,3072]{1,0:T(8,128)}, f32[768,768]{1,0:T(8,128)}), (f32[32,4608]{0,1:T(8,128)}, f32[192,2304]{1,0:T(8,128)}, ...) | async-done | bytes 7667728 | tf_op jit(solution)/shard_map/psum | solution.py:296
  (328 shorter events, 213.3 us)
Async XLA Ops:
  7.2 6.7 copy-start
  7.2 6.6 copy-start.10
  7.2 5.1 copy-start.14
  8.1 5.1 copy-start.35
  34.5 111.3 %all-to-all-start = ((bf16[4,256,3,768]{1,0,2,3:T(4,128)(2,1)}), bf16[4,256,3,768]{1,0,2,3:T(4,128)(2,1)}, u32[]{:S(2)}, u32[]{:S(2)}) async-start(bf16[4,256,3,768]{1,0,2,3:T(4,128)(2,1)} %copy.122), calls=%async_computation | async-start | bytes 9437184 | tf_op jit(solution)/shard_map/all_to_all | solution.py:166
  257.5 56.4 %copy-start.31 = (f32[4,768]{1,0:T(4,128)S(1)}, f32[4,768]{1,0:T(4,128)}, u32[]{:S(2)}) copy-start(f32[4,768]{1,0:T(4,128)} %get-tuple-element.262) | copy-start | bytes 36868
  257.5 52.3 %all-to-all-start.1 = ((bf16[4,1024,192]{2,0,1:T(4,128)(2,1)}), bf16[4,1024,192]{2,0,1:T(4,128)(2,1)}, u32[]{:S(2)}, u32[]{:S(2)}) async-start(bf16[4,1024,192]{2,0,1:T(4,128)(2,1)} %copy.125), calls=%async_computation.1 | async-start | bytes 4194304 | tf_op jit(solution)/shard_map/all_to_all | solution.py:168
  262.1 559.2 %reduce-scatter.16.cloned.1.call-start = ((), (), s32[]{:S(2)}) async-start(), calls=%async_computation.13 | async-start | bytes 2949120
  263.1 92.7 %copy-start.24 = (f32[768]{0:T(1024)}, f32[768]{0:T(1024)S(1)}, u32[]{:S(2)}) copy-start(f32[768]{0:T(1024)S(1)} %convert_element_type.129) | copy-start | bytes 9220
  318.0 37.7 %copy-start.8 = (f32[4,256,768]{2,1,0:T(8,128)}, f32[4,256,768]{2,1,0:T(8,128)S(1)}, u32[]{:S(2)}) copy-start(f32[4,256,768]{2,1,0:T(8,128)S(1)} %get-tuple-element.217) | copy-start | bytes 9437188
  318.1 37.7 %copy-start.26 = (f32[4,256]{1,0:T(4,128)}, f32[4,256]{1,0:T(4,128)S(1)}, u32[]{:S(2)}) copy-start(f32[4,256]{1,0:T(4,128)S(1)} %broadcast_multiply_fusion.6) | copy-start | bytes 12292
  318.6 37.2 %copy-start.27 = (f32[4,256]{1,0:T(4,128)}, f32[4,256]{1,0:T(4,128)S(1)}, u32[]{:S(2)}) copy-start(f32[4,256]{1,0:T(4,128)S(1)} %add_rsqrt_fusion) | copy-start | bytes 12292
  318.8 8.2 copy-start.38
  318.8 8.2 copy-start.40
  318.8 8.2 copy-start.49
  342.8 13.0 copy-start.13
  342.8 13.0 copy-start.46
  355.8 17.1 %copy-start.18 = (bf16[768,768]{1,0:T(8,128)(2,1)S(1)}, bf16[768,768]{1,0:T(8,128)(2,1)}, u32[]{:S(2)}) copy-start(bf16[768,768]{1,0:T(8,128)(2,1)} %param.23) | copy-start | bytes 3538948
  439.3 8.3 copy-start.1
  439.3 8.3 copy-start.11
  439.3 8.4 copy-start.12
  453.2 6.7 copy-start.4
  481.4 8.3 copy-start.1
  481.4 8.3 copy-start.11
  481.4 8.4 copy-start.12
  495.3 6.7 copy-start.4
  523.5 8.3 copy-start.1
  523.5 8.3 copy-start.11
  523.5 8.4 copy-start.12
  537.4 6.7 copy-start.4
  565.6 8.3 copy-start.1
  565.6 8.3 copy-start.11
  565.6 8.4 copy-start.12
  579.5 6.7 copy-start.4
  746.5 10.3 copy-start.29
  746.5 10.3 copy-start.33
  756.7 10.0 copy-start.44
  756.7 10.0 copy-start.42
  756.7 10.0 copy-start.41
  756.8 10.0 copy-start.43
  756.8 10.6 copy-start.48
  773.9 5.3 copy-start.20
  773.9 5.3 copy-start.25
  773.9 97.2 %reduce-scatter.10.cloned.1.call-start = ((), (), s32[]{:S(2)}) async-start(), calls=%async_computation.10 | async-start | bytes 2949120 | tf_op jit(solution)/shard_map/reduce_scatter | solution.py:289
  779.1 255.2 %reduce-scatter.12.cloned.1.call-start = ((), (), s32[]{:S(2)}) async-start(), calls=%async_computation.11 | async-start | bytes 11796480 | tf_op jit(solution)/shard_map/reduce_scatter | solution.py:291
  790.1 408.6 %reduce-scatter.14.cloned.1.call-start = ((), (), s32[]{:S(2)}) async-start(), calls=%async_computation.12 | async-start | bytes 11796480 | tf_op jit(solution)/shard_map/reduce_scatter | solution.py:293
  804.8 520.4 %reduce-scatter.8.cloned.1.call-start = ((), (), s32[]{:S(2)}) async-start(), calls=%async_computation.9 | async-start | bytes 8847360 | tf_op jit(solution)/shard_map/reduce_scatter | solution.py:288
  815.7 654.7 %all-reduce.10.cloned.1.call-start = ((), (), s32[]{:S(2)}) async-start(), calls=%async_computation.14 | async-start | bytes 18874368 | tf_op jit(solution)/shard_map/psum | solution.py:296
  (42 other events, 87.3 us)
Sparse Core Ops, SparseCore 0:
  774.0 47.2 reduce-scatter.15
  823.6 47.5 reduce-scatter.9
  873.5 160.7 reduce-scatter.11
  1036.5 162.1 reduce-scatter.13
  1200.8 124.3 reduce-scatter.7
  1329.9 140.4 all-reduce.9
where the time goes:
time: 1500 us; the launch traced here: 1490 us
  waiting for transfers between devices  716 us (48%)
  matrix products  284 us (19%)
  blocking collectives  246 us (16%)
  local copies, waits for them, and re-layouts  137 us (9%)
  other arithmetic  74.4 us (5%)
  between operations  16.9 us (1%)
    reduce_scatter x1, waiting for transfers between devices, body(): lax.psum_scatter(grad_down_weight, 'sp', scatter_dimension=0, tiled=True)  164 us
    reduce_scatter x1, waiting for transfers between devices, body(): lax.psum_scatter(grad_up_weight, 'sp', scatter_dimension=0, tiled=True)  163 us
    all_to_all x1, blocking collectives, body(): lax.all_to_all(grad_qkv_heads, 'sp', split_axis=1, concat_axis=3, tiled=T...  144 us
    reduce_scatter x1, waiting for transfers between devices, body(): lax.psum_scatter(grad_qkv_weight, 'sp', scatter_dimension=0, tiled=True)  127 us
    all_to_all x1, waiting for transfers between devices, body(): lax.all_to_all(qkv_seq, 'sp', split_axis=3, concat_axis=1, tiled=True)  103 us
    psum x1, waiting for transfers between devices, body(): lax.psum((shards[0], shards[1], shards[2], shards[3], shards[4], shards[5...  62.5 us
    reduce_scatter x1, waiting for transfers between devices, body(): lax.psum_scatter(grad_proj_weight, 'sp', scatter_dimension=0, tiled=True)  46.7 us
    all_to_all x1, waiting for transfers between devices, body(): lax.all_to_all(mixed_heads, 'sp', split_axis=1, concat_axis=2, tiled=True)  44.1 us
  transfers between devices with their start and end apart: 8, of which 8 were waited for; matrix products, arithmetic and copies ran while one was open for 5% of the time, Pallas kernels for 0%

commit v1 on v0

--- a/solution.py
+++ b/solution.py
@@ -245,8 +245,11 @@
         return backward_single(pair[0], pair[1], cos_table, sin_table)
 
     grad_qkv_heads = lax.map(kept_pair, (kept_heads, grad_heads))
-    query_key_value_gradient = lax.all_to_all(
-        grad_qkv_heads, "sp", split_axis=1, concat_axis=3, tiled=True
+    query_key_value_gradient = jnp.concatenate(
+        lax.all_to_all(
+            jnp.stack(jnp.split(grad_qkv_heads, lax.axis_size("sp"), axis=1)), "sp", 0, 0
+        ),
+        axis=3,
     ).reshape(seq_count, local_len, 3 * width)
     grad_qkv_weight = jnp.einsum(
         "kuv,kuf->vf",

time: 1500 us -> 1440 us (0.960)
  blocking collectives: 246 us -> 208 us
  local copies, waits for them, and re-layouts: 137 us -> 121 us
    all_to_all x1, blocking collectives: 144 us -> 107 us  [body(): lax.all_to_all(jnp.stack(jnp.split(grad_qkv_heads, lax.axis_size('sp'), a...]
where the time goes in v1:
time: 1440 us; the launch traced here: 1430 us
  waiting for transfers between devices  716 us (50%)
  matrix products  281 us (20%)
  blocking collectives  208 us (14%)
  local copies, waits for them, and re-layouts  121 us (8%)
  other arithmetic  75.1 us (5%)
  between operations  17 us (1%)
    reduce_scatter x1, waiting for transfers between devices, body(): lax.psum_scatter(grad_down_weight, 'sp', scatter_dimension=0, tiled=True)  164 us
    reduce_scatter x1, waiting for transfers between devices, body(): lax.psum_scatter(grad_up_weight, 'sp', scatter_dimension=0, tiled=True)  163 us
    reduce_scatter x1, waiting for transfers between devices, body(): lax.psum_scatter(grad_qkv_weight, 'sp', scatter_dimension=0, tiled=True)  126 us
    all_to_all x1, blocking collectives, body(): lax.all_to_all(jnp.stack(jnp.split(grad_qkv_heads, lax.axis_size('sp'), a...  107 us
    all_to_all x1, waiting for transfers between devices, body(): lax.all_to_all(qkv_seq, 'sp', split_axis=3, concat_axis=1, tiled=True)  103 us
    psum x1, waiting for transfers between devices, body(): lax.psum((shards[0], shards[1], shards[2], shards[3], shards[4], shards[5...  62.5 us
    reduce_scatter x1, waiting for transfers between devices, body(): lax.psum_scatter(grad_proj_weight, 'sp', scatter_dimension=0, tiled=True)  46.7 us
    all_to_all x1, waiting for transfers between devices, body(): lax.all_to_all(mixed_heads, 'sp', split_axis=1, concat_axis=2, tiled=True)  44.1 us
  transfers between devices with their start and end apart: 8, of which 8 were waited for; matrix products, arithmetic and copies ran while one was open for 5% of the time, Pallas kernels for 0%

profile of v1, /device:TPU:0, one launch (start us, length us, event | category | flops | bytes accessed | tf_op | source)
XLA Modules:
  0.0 1431.8 jit_solution(4447755043486313630)
XLA Ops:
  13.8 5.8 convolution_convert_fusion
  19.7 6.7 copy.116
  26.3 8.1 copy.117
  34.5 6.5 all-to-all-start
  42.4 103.3 %all-to-all-done = bf16[4,256,3,768]{1,0,2,3:T(4,128)(2,1)} async-done(((bf16[4,256,3,768]{1,0,2,3:T(4,128)(2,1)}), bf16[4,256,3,768]{1,0,2,3:T(4,128)(2,1)}, u32[]{:S(2)}, u32[]{:S(2)}) %all-to-all-start) | async-done | bytes 4718624 | tf_op jit(solution)/shard_map/all_to_all | solution.py:166
  154.3 99.2 %while.22 = (s32[]{:T(128)}, bf16[4,1024,192]{1,2,0:T(8,128)(2,1)}, bf16[4,1024,3,192]{1,3,2,0:T(8,128)(2,1)}, bf16[4,1024,3,192]{1,3,2,0:T(8,128)(2,1)}, f32[10...) while((s32[]{:T(128)}, bf16[4,1024,192]{1,2,0:T(8,128)(2,1)}, ...), condition=%wide.region_5.6_spmd, body=%wide.region_2.5_spmd.sunk | while | flops 828703744 | bytes 63856824 | solution.py:85
  162.8 9.6 fusion.151
  172.4 5.9 fusion.152
  187.6 9.6 fusion.151
  197.2 5.9 fusion.152
  212.4 9.6 fusion.151
  222.0 5.9 fusion.152
  237.2 9.6 fusion.151
  246.8 5.9 fusion.152
  265.8 44.1 %all-to-all-done.1 = bf16[4,1024,192]{2,0,1:T(4,128)(2,1)} async-done(((bf16[4,1024,192]{2,0,1:T(4,128)(2,1)}), bf16[4,1024,192]{2,0,1:T(4,128)(2,1)}, u32[]{:S(2)}, u32[]{:S(2)}) %all-to-all-start.1) | async-done | bytes 1572896 | tf_op jit(solution)/shard_map/all_to_all | solution.py:168
  318.9 8.2 fusion.44
  327.1 15.7 %convert_reduce_fusion = (f32[3072]{0:T(1024)}, bf16[4,256,3072]{2,1,0:T(8,128)(2,1)S(1)}) fusion(f32[4,256,3072]{2,1,0:T(8,128)} %fusion.44, f32[3072]{0:T(1024)S(1)} %copy-done.44, bf16[3072,768]{1,0:T(8,128)(2,1)} %param.27, bf16[4,256,768]{2,1,0:T(8,128)(2,1)S(1)} %copy-done.53, f32[4,768]{1,0:T(4,128)S(1)} %copy-done.42), kind=kOutput, calls=%fused_computation.65 | convolution fusion | flops 4906546176 | bytes 25202688 | tf_op jit(solution)/shard_map/eoa,ta->eot/dot_general | solution.py:201
  342.9 13.0 multiply_reduce_fusion.3
  355.9 15.4 %convert_reduce_fusion.2 = (f32[768]{0:T(1024)}, f32[4,768]{1,0:T(4,128)}, bf16[4,256,768]{2,1,0:T(8,128)(2,1)}, f32[4,768]{1,0:T(4,128)}, f32[4,256,768]{2,1,0:T(8,128)S(1)}) fusion(bf16[4,256,768]{2,1,0:T(8,128)(2,1)S(1)} %copy-done.53, f32[4,768]{1,0:T(4,128)S(1)} %copy-done.42, f32[768]{0:T(1024)S(1)} %copy-done.50, ...), kind=kOutput, calls=%fused_computation.112 | convolution fusion | flops 4880589824 | bytes 33117184 | tf_op jit(solution)/shard_map/ngw,wo->ngo/dot_general | solution.py:190
  379.3 40.1 %all_to_all.59 = bf16[4,256,768]{1,0,2:T(4,128)(2,1)S(1)} all-to-all(bf16[4,256,768]{1,0,2:T(4,128)(2,1)} %copy.124), channel_id=1, replica_groups=mesh['dp'=8,'sp'=4] {'sp'}, dimensions={2} | all-to-all | bytes 3145728 | tf_op jit(solution)/shard_map/all_to_all | solution.py:241
  423.7 168.6 %while.23 = (s32[]{:T(128)}, bf16[4,1024,3,192]{1,3,2,0:T(8,128)(2,1)}, bf16[4,1024,3,192]{1,3,2,0:T(8,128)(2,1)}, bf16[4,1024,192]{1,2,0:T(8,128)(2,1)}, f32[10...) while((s32[]{:T(128)}, bf16[4,1024,3,192]{1,3,2,0:T(8,128)(2,1)}, ...), condition=%wide.region_14.15_spmd, body=%wide.region_10.0_spmd.sunk | while | flops 2057041920 | bytes 176759088 | solution.py:247
  429.8 9.5 fusion.167
  439.3 6.9 fusion.168
  453.3 6.7 multiply_convert_fusion.8
  471.9 9.5 fusion.167
  481.5 6.9 fusion.168
  489.9 5.6 multiply_reduce_fusion.9
  495.5 6.7 multiply_convert_fusion.8
  514.1 9.6 fusion.167
  523.6 6.9 fusion.168
  532.0 5.6 multiply_reduce_fusion.9
  537.6 6.7 multiply_convert_fusion.8
  556.2 9.6 fusion.167
  565.8 6.9 fusion.168
  579.8 6.7 multiply_convert_fusion.8
  595.9 106.6 %all_to_all.60 = bf16[4,4,256,3,192]{2,4,3,1,0:T(8,128)(2,1)S(1)} all-to-all(bf16[4,4,256,3,192]{2,4,3,1,0:T(8,128)(2,1)S(1)} %pad_maximum_fusion), channel_id=1, replica_groups=mesh['dp'=8,'sp'=4] {'sp'}, dimensions={0} | all-to-all | bytes 9437184 | tf_op jit(solution)/shard_map/all_to_all | solution.py:249
  704.0 7.2 fusion.67
  723.8 10.9 convolution_bitcast_fusion.4
  735.4 13.7 convolution_bitcast_fusion.3
  749.8 10.2 convolution_bitcast_fusion.5
  768.8 46.7 %reduce-scatter.10.cloned.1.call-done = f32[192,768]{1,0:T(8,128)} async-done(((f32[768,768]{1,0:T(8,128)}), f32[192,768]{1,0:T(8,128)}) %reduce-scatter.10.cloned.1.call-update) | async-done | bytes 589840 | tf_op jit(solution)/shard_map/reduce_scatter | solution.py:292
  815.6 163.2 %reduce-scatter.12.cloned.1.call-done = f32[192,3072]{1,0:T(8,128)} async-done(((f32[768,3072]{1,0:T(8,128)}), f32[192,3072]{1,0:T(8,128)}) %reduce-scatter.12.cloned.1.call-update) | async-done | bytes 2359312 | tf_op jit(solution)/shard_map/reduce_scatter | solution.py:294
  978.7 164.4 %reduce-scatter.14.cloned.1.call-done = f32[768,768]{1,0:T(8,128)} async-done(((f32[3072,768]{1,0:T(8,128)}), f32[768,768]{1,0:T(8,128)}) %reduce-scatter.14.cloned.1.call-update) | async-done | bytes 2359312 | tf_op jit(solution)/shard_map/reduce_scatter | solution.py:296
  1143.1 126.5 %reduce-scatter.8.cloned.1.call-done = f32[192,2304]{1,0:T(8,128)} async-done(((f32[768,2304]{1,0:T(8,128)}), f32[192,2304]{1,0:T(8,128)}) %reduce-scatter.8.cloned.1.call-update) | async-done | bytes 1769488 | tf_op jit(solution)/shard_map/reduce_scatter | solution.py:291
  1275.0 19.8 %all-reduce.7 = (f32[4608]{0:T(1024)}, f32[768]{0:T(1024)}, f32[768]{0:T(1024)}, f32[3072]{0:T(1024)}, f32[768]{0:T(1024)}) all-reduce(f32[4608]{0:T(1024)} %get-tuple-element.259, f32[768]{0:T(1024)} %get-tuple-element.162, f32[768]{0:T(1024)} %get-tuple-element.159, ...), channel_id=3, replica_groups=mesh['dp'=8,'sp'=4] {'sp'}, use_global_device_ids=true, to_apply=%region_27.28.clone | all-reduce | flops 9984 | bytes 79872
  1301.5 24.7 %all-reduce.5 = (f32[1152]{0:T(1024)}, f32[192]{0:T(256)}, f32[192]{0:T(256)}, f32[768]{0:T(1024)}, f32[192]{0:T(256)}) all-reduce(f32[1152]{0:T(1024)} %dynamic-slice.1, f32[192]{0:T(256)} %dynamic-slice.3, f32[192]{0:T(256)} %dynamic-slice.5, f32[768]{0:T(1024)} %dynamic-slice.7, ...), channel_id=1, replica_groups=mesh['dp'=8,'sp'=4] {'dp'}, use_global_device_ids=true, to_apply=%region_28.29 | all-reduce | flops 2496 | bytes 19968 | tf_op jit(solution)/shard_map/psum | solution.py:299
  1326.2 17.2 %psum.77 = bf16[4,4608]{1,0:T(4,128)(2,1)} all-reduce(bf16[4,4608]{1,0:T(4,128)(2,1)} %get-tuple-element.260), channel_id=1, replica_groups=mesh['dp'=8,'sp'=4] {'sp'}, use_global_device_ids=true, to_apply=%region_23.24 | all-reduce | flops 18432 | bytes 73728 | tf_op jit(solution)/shard_map/psum | solution.py:283
  1352.3 62.5 %all-reduce.10.cloned.1.call-done = (f32[32,4608]{0,1:T(8,128)}, f32[192,2304]{1,0:T(8,128)}, f32[192,768]{1,0:T(8,128)}, f32[192,3072]{1,0:T(8,128)}, f32[768,768]{1,0:T(8,128)}) async-done(((f32[32,4608]{0,1:T(8,128)}, f32[192,2304]{1,0:T(8,128)}, f32[192,768]{1,0:T(8,128)}, f32[192,3072]{1,0:T(8,128)}, f32[768,768]{1,0:T(8,128)}), (f32[32,4608]{0,1:T(8,128)}, f32[192,2304]{1,0:T(8,128)}, ...) | async-done | bytes 7667728 | tf_op jit(solution)/shard_map/psum | solution.py:299
  (337 shorter events, 207.3 us)
Async XLA Ops:
  7.2 6.6 copy-start
  7.2 6.6 copy-start.10
  7.2 5.1 copy-start.16
  7.2 5.1 copy-start.51
  8.1 5.1 copy-start.37
  34.5 111.3 %all-to-all-start = ((bf16[4,256,3,768]{1,0,2,3:T(4,128)(2,1)}), bf16[4,256,3,768]{1,0,2,3:T(4,128)(2,1)}, u32[]{:S(2)}, u32[]{:S(2)}) async-start(bf16[4,256,3,768]{1,0,2,3:T(4,128)(2,1)} %copy.117), calls=%async_computation | async-start | bytes 9437184 | tf_op jit(solution)/shard_map/all_to_all | solution.py:166
  257.6 56.4 %copy-start.33 = (f32[4,768]{1,0:T(4,128)S(1)}, f32[4,768]{1,0:T(4,128)}, u32[]{:S(2)}) copy-start(f32[4,768]{1,0:T(4,128)} %get-tuple-element.266) | copy-start | bytes 36868
  257.6 52.3 %all-to-all-start.1 = ((bf16[4,1024,192]{2,0,1:T(4,128)(2,1)}), bf16[4,1024,192]{2,0,1:T(4,128)(2,1)}, u32[]{:S(2)}, u32[]{:S(2)}) async-start(bf16[4,1024,192]{2,0,1:T(4,128)(2,1)} %copy.120), calls=%async_computation.1 | async-start | bytes 4194304 | tf_op jit(solution)/shard_map/all_to_all | solution.py:168
  262.2 503.5 %reduce-scatter.16.cloned.1.call-start = ((), (), s32[]{:S(2)}) async-start(), calls=%async_computation.13 | async-start | bytes 2949120
  263.2 92.7 %copy-start.26 = (f32[768]{0:T(1024)}, f32[768]{0:T(1024)S(1)}, u32[]{:S(2)}) copy-start(f32[768]{0:T(1024)S(1)} %convert_element_type.129) | copy-start | bytes 9220
  318.1 37.7 %copy-start.8 = (f32[4,256,768]{2,1,0:T(8,128)}, f32[4,256,768]{2,1,0:T(8,128)S(1)}, u32[]{:S(2)}) copy-start(f32[4,256,768]{2,1,0:T(8,128)S(1)} %get-tuple-element.217) | copy-start | bytes 9437188
  318.2 37.7 %copy-start.28 = (f32[4,256]{1,0:T(4,128)}, f32[4,256]{1,0:T(4,128)S(1)}, u32[]{:S(2)}) copy-start(f32[4,256]{1,0:T(4,128)S(1)} %broadcast_multiply_fusion.6) | copy-start | bytes 12292
  318.7 37.2 %copy-start.29 = (f32[4,256]{1,0:T(4,128)}, f32[4,256]{1,0:T(4,128)S(1)}, u32[]{:S(2)}) copy-start(f32[4,256]{1,0:T(4,128)S(1)} %add_rsqrt_fusion) | copy-start | bytes 12292
  318.9 8.2 copy-start.42
  318.9 8.2 copy-start.44
  318.9 8.2 copy-start.53
  342.8 13.0 copy-start.14
  342.8 13.0 copy-start.50
  355.9 17.1 %copy-start.20 = (bf16[768,768]{1,0:T(8,128)(2,1)S(1)}, bf16[768,768]{1,0:T(8,128)(2,1)}, u32[]{:S(2)}) copy-start(bf16[768,768]{1,0:T(8,128)(2,1)} %param.23) | copy-start | bytes 3538948
  439.3 8.3 copy-start.1
  439.3 8.3 copy-start.12
  439.3 8.4 copy-start.13
  453.3 6.7 copy-start.4
  481.5 8.3 copy-start.1
  481.5 8.3 copy-start.12
  481.5 8.4 copy-start.13
  495.5 6.7 copy-start.4
  523.6 8.3 copy-start.1
  523.6 8.3 copy-start.12
  523.6 8.4 copy-start.13
  537.6 6.7 copy-start.4
  565.7 8.3 copy-start.1
  565.8 8.3 copy-start.12
  565.8 8.4 copy-start.13
  579.8 6.7 copy-start.4
  703.1 8.2 copy-start.15
  704.0 7.3 copy-start.48
  704.0 7.3 copy-start.46
  704.0 7.3 copy-start.45
  704.0 7.3 copy-start.47
  704.0 8.0 copy-start.52
  718.5 5.3 copy-start.22
  718.5 5.3 copy-start.27
  718.5 97.0 %reduce-scatter.10.cloned.1.call-start = ((), (), s32[]{:S(2)}) async-start(), calls=%async_computation.10 | async-start | bytes 2949120 | tf_op jit(solution)/shard_map/reduce_scatter | solution.py:292
  723.7 255.0 %reduce-scatter.12.cloned.1.call-start = ((), (), s32[]{:S(2)}) async-start(), calls=%async_computation.11 | async-start | bytes 11796480 | tf_op jit(solution)/shard_map/reduce_scatter | solution.py:294
  734.7 408.4 %reduce-scatter.14.cloned.1.call-start = ((), (), s32[]{:S(2)}) async-start(), calls=%async_computation.12 | async-start | bytes 11796480 | tf_op jit(solution)/shard_map/reduce_scatter | solution.py:296
  749.1 520.5 %reduce-scatter.8.cloned.1.call-start = ((), (), s32[]{:S(2)}) async-start(), calls=%async_computation.9 | async-start | bytes 8847360 | tf_op jit(solution)/shard_map/reduce_scatter | solution.py:291
  760.0 654.8 %all-reduce.10.cloned.1.call-start = ((), (), s32[]{:S(2)}) async-start(), calls=%async_computation.14 | async-start | bytes 18874368 | tf_op jit(solution)/shard_map/psum | solution.py:299
  (46 other events, 89.3 us)
Sparse Core Ops, SparseCore 0:
  718.6 46.9 reduce-scatter.15
  768.0 47.5 reduce-scatter.9
  817.9 160.7 reduce-scatter.11
  980.9 162.1 reduce-scatter.13
  1145.2 124.2 reduce-scatter.7
  1274.3 140.4 all-reduce.9
